TPU v7x, 512 devices: a whole 4x8x8 slice. The times are simulated.
512 devices in a mesh: segment: 4 (over x), shard: 128 (over z, y, core).
Axes of the slice: x: 4, y: 8, z: 8, core: 2. Of those that a mesh axis runs over, the one named last changes fastest.
Arguments:
- proposal_attributes: bfloat16 [2, 65536, 1024], P(None, 'shard'), may hold values from -6 to 6
- keeper_ordering_vectors: bfloat16 [2, 16384, 4096], P(None, 'shard'), may hold values from -6 to 6
- keeper_positions: int32 [2, 16384], P(None, 'shard'), may hold values from 0 to 511
- alive_tallies: int32 [2, 128], P(None, 'shard'), may hold values from 256 to 512
- holder_shards: int32 [2, 16384, 1], P(None, 'shard'), may hold values from 0 to 127; in each aligned block of 128 rows (0 to 127, 128 to 255, ..., all dimensions but the last counted through in order) at most 2 rows name the same one
- holder_attribute_factor: bfloat16 [128, 4096], P('shard'), may hold values from 0.099609375 to 1.8984375
- early_inner_matrix: bfloat16 [1024, 1024], replicated, may hold values from -0.1875 to 0.1875
- early_inner_offset: float32 [1024], replicated, may hold values from -3 to 3
- early_grading_vector: bfloat16 [1024], replicated, may hold values from -0.1875 to 0.1875
- block_lowering_matrices: bfloat16 [3, 4096, 128], P(None, 'shard'), may hold values from -0.09375 to 0.09375
- block_raising_flipped: bfloat16 [3, 4096, 128], P(None, 'shard'), may hold values from -0.5 to 0.5
- block_result_offsets: float32 [3, 4096], replicated, may hold values from -3 to 3
- block_grading_vectors: float32 [3, 4096], replicated, may hold values from -0.09375 to 0.09375
Outputs:
- exits: float32 [4, 2, 32768], P('segment', None, 'shard')
Inputs may be any that keep to these rules, and one draw needn't show every extreme that they name: `holder_shards`: in every round at most 2 entries of one block of 128 go to one owner. `keeper_positions`: entries at or above the block's count in alive_tallies are padding.
All inputs are finite; a program needn't handle non-finite values.
Results may differ from a plain program's by a relative error of at most 0.02.
Values may be sent and summed in bfloat16 or wider, within the bound.
A program may use at most 64 MiB of HBM per device.

v0:
```python
import jax
import jax.numpy as jnp
from jax import lax
from jax.sharding import PartitionSpec as P

F32 = jnp.float32
BF16 = jnp.bfloat16
HIGH = lax.Precision.HIGHEST
LANES = 128


def fdot(a, b, precision=None):
    return jnp.dot(a, b, preferred_element_type=F32, precision=precision)


def gather_blocks(block):
    return lax.all_gather(block, "shard", axis=0, tiled=False)


def sum_segments(value):
    return lax.psum(value, "segment")


def local(
    proposal_attributes,
    keeper_ordering_vectors,
    keeper_positions,
    alive_tallies,
    holder_shards,
    holder_attribute_factor,
    early_inner_matrix,
    early_inner_offset,
    early_grading_vector,
    block_lowering_matrices,
    block_raising_flipped,
    block_result_offsets,
    block_grading_vectors,
):
    segment_id = lax.axis_index("segment")
    segment_count = lax.axis_size("segment")
    shard_count = lax.axis_size("shard")
    rounds, entries, width = keeper_ordering_vectors.shape
    candidates = proposal_attributes.shape[1]
    low_rank = block_lowering_matrices.shape[2]
    cap_slots = max(2, 2 * entries // shard_count)
    rows = rounds * entries
    own_features = width // shard_count
    piece = own_features // segment_count
    part_width = width // segment_count
    span = segment_count * LANES
    spans = width // span
    at = lax.broadcasted_iota(jnp.int32, (span, LANES), 0)
    to = lax.broadcasted_iota(jnp.int32, (span, LANES), 1)
    chosen = (at // own_features == to // piece) & (
        at % own_features == segment_id * piece + to % piece
    )
    pick = chosen.astype(BF16)
    pick32 = chosen.astype(F32)

    def part_of(values):
        return [fdot(values[:, g * span : (g + 1) * span], pick) for g in range(spans)]

    def part_of32(values):
        return jnp.concatenate(
            [fdot(values[:, g * span : (g + 1) * span], pick32, HIGH) for g in range(spans)], 1
        )

    own_gain = jnp.concatenate(part_of(holder_attribute_factor), 0).astype(BF16)
    own_lower = lax.dynamic_slice_in_dim(block_lowering_matrices, segment_id * piece, piece, 1)
    own_raise = lax.dynamic_slice_in_dim(block_raising_flipped, segment_id * piece, piece, 1)
    block = jnp.concatenate(
        [own_lower.reshape(3 * piece, low_rank), own_raise.reshape(3 * piece, low_rank), own_gain],
        0,
    )
    blocks = gather_blocks(block)

    def matrix(k):
        return blocks[:, k * piece : (k + 1) * piece].reshape(part_width, low_rank)

    hidden = jax.nn.relu(
        fdot(proposal_attributes.reshape(rounds * candidates, -1), early_inner_matrix)
        + early_inner_offset
    ).astype(BF16)
    scores = fdot(hidden, early_grading_vector).reshape(rounds, candidates)
    ids = jnp.arange(candidates, dtype=jnp.int32)
    looked_up = jnp.sum(
        jnp.where(keeper_positions[:, :, None] == ids, scores[:, None, :], 0.0), axis=2
    )
    keep = (keeper_positions < alive_tallies).astype(F32)
    gate = jax.nn.sigmoid(looked_up) * keep
    owner = holder_shards[:, :, 0]
    order = jnp.arange(entries, dtype=jnp.int32)
    same = (owner[:, :, None] == owner[:, None, :]) & (order[None, :] < order[:, None])
    within = jnp.sum(same.astype(jnp.int32), axis=2)
    target = owner * cap_slots + within
    slots = jnp.arange(shard_count * cap_slots, dtype=jnp.int32)
    placed = slots[None, :, None] == target[:, None, :]
    gate_col = gate.reshape(rows, 1)
    keep_col = keep.reshape(rows, 1)
    own_rows = jnp.concatenate(part_of(keeper_ordering_vectors.reshape(rows, width)), 1)
    h0 = (own_rows * gate_col).astype(BF16)
    owner_hot = (
        owner.reshape(rows, 1) == jnp.arange(shard_count, dtype=jnp.int32)[None, :]
    ).astype(BF16)
    gains = jnp.concatenate(
        [fdot(owner_hot, blocks[:, 6 * piece + g]) for g in range(part_width // LANES)], 1
    )
    x = (h0.astype(F32) * gains).astype(BF16)
    biases = part_of32(block_result_offsets)
    heads = part_of32(block_grading_vectors)
    lower1, lower2, lower3, raise1, raise2, raise3 = [matrix(k) for k in range(6)]
    between = lax.dot_general(raise2, lower3, (((0,), (0,)), ((), ())), preferred_element_type=F32)
    raised = lax.dot_general(
        heads[1:3], raise2.astype(F32), (((1,), (0,)), ((), ())), precision=HIGH
    )
    raised3 = lax.dot_general(
        heads[2:3], raise3.astype(F32), (((1,), (0,)), ((), ())), precision=HIGH
    )
    lowered_bias = lax.dot_general(
        biases[1:2], lower3.astype(F32), (((1,), (0,)), ((), ())), precision=HIGH
    )
    consts = jnp.stack(
        [
            jnp.sum(biases[1] * heads[1]),
            jnp.sum(biases[1] * heads[2]),
            jnp.sum(biases[2] * heads[2]),
        ]
    )
    consts = jnp.pad(consts, (0, low_rank - 3))[None]
    first = jnp.concatenate([fdot(x, lower1), between, raised, raised3, lowered_bias, consts], 0)
    first = sum_segments(jnp.pad(first, ((0, 3), (0, 0))))
    act1 = first[:rows].astype(BF16)
    lifted = (
        lax.dot_general(act1, raise1, (((1,), (1,)), ((), ())), preferred_element_type=F32)
        + biases[0]
    )
    x32 = x.astype(F32)
    out1 = (x32 + x32 * lifted) * keep_col
    h1 = out1.astype(BF16)
    h1_32 = h1.astype(F32)
    graded = jnp.stack(
        [
            jnp.sum(out1 * heads[0], axis=1),
            jnp.sum(h1_32 * heads[1], axis=1),
            jnp.sum(h1_32 * heads[2], axis=1),
        ]
    ).reshape(-1, low_rank)
    second = jnp.concatenate([fdot(h1, lower2), fdot(h1, lower3), graded], 0)
    second = sum_segments(jnp.pad(second, ((0, -second.shape[0] % 8), (0, 0))))
    between = first[rows : rows + low_rank]
    vectors = first[rows + low_rank : rows + low_rank + 5]
    graded = second[2 * rows : 2 * rows + 3 * rows // low_rank].reshape(3, rows)
    keep_row = keep.reshape(rows)
    act2 = jax.nn.relu(second[:rows]).astype(BF16).astype(F32)
    graded2 = graded[1] + jnp.sum(act2 * vectors[0], axis=1) + vectors[4, 0]
    inner3 = (second[rows : 2 * rows] + fdot(act2, between, HIGH) + vectors[3]) * keep_col
    act3 = jax.nn.relu(inner3).astype(BF16).astype(F32)
    graded3 = (
        (graded[2] + jnp.sum(act2 * vectors[1], axis=1) + vectors[4, 1]) * keep_row
        + jnp.sum(act3 * vectors[2], axis=1)
        + vectors[4, 2]
    )
    section = jnp.stack([gate.reshape(rows), graded[0], graded2 * keep_row, graded3 * keep_row])
    values = lax.dynamic_index_in_dim(section, segment_id, 0, keepdims=False)
    values = values.reshape(rounds, 1, entries)
    sent = jnp.sum(jnp.where(placed, values, 0.0), axis=2)
    outgoing = sent.reshape(rounds, shard_count, cap_slots).transpose(1, 0, 2)
    outgoing = outgoing.reshape(shard_count, rounds * cap_slots)
    arrived = lax.all_to_all(outgoing, "shard", split_axis=0, concat_axis=0, tiled=True)
    arrived = arrived.reshape(shard_count, rounds, cap_slots).transpose(1, 0, 2)
    arrived = arrived.reshape(rounds, shard_count * cap_slots)
    return jnp.where(segment_id == 0, sent, arrived)[None]


def solution(mesh):
    placed = (
        P(None, "shard", None),
        P(None, "shard", None),
        P(None, "shard"),
        P(None, "shard"),
        P(None, "shard", None),
        P("shard", None),
        P(),
        P(),
        P(),
        P(None, "shard", None),
        P(None, "shard", None),
        P(),
        P(),
    )
    return jax.shard_map(
        local, mesh=mesh, in_specs=placed, out_specs=P("segment", None, "shard"), check_vma=False
    )
```

profile of v0, /device:TPU:1, one launch (start us, length us, event | category | flops | bytes accessed | tf_op | source)
XLA Modules:
  0.0 260.8 jit_solution(11579320052899533610)
XLA Ops:
  7.3 0.8 fusion.38
  8.1 0.8 fusion.40
  8.9 0.8 fusion.42
  9.7 0.8 fusion.44
  10.6 0.8 fusion.46
  11.4 0.8 fusion.48
  14.6 1.8 concatenate.25
  17.2 0.9 fusion.28
  18.0 0.9 fusion.27
  18.9 0.9 fusion.26
  19.8 0.9 fusion.25
  20.7 0.9 fusion.24
  21.6 0.9 fusion.23
  22.5 0.9 fusion.22
  23.4 0.9 fusion.21
  24.3 0.9 fusion.36
  25.1 0.9 fusion.35
  26.0 0.9 fusion.34
  26.9 0.9 fusion.33
  27.8 0.9 fusion.32
  28.7 0.9 fusion.31
  29.6 4.4 %fusion = f32[1,1024]{1,0:T(1,128)S(1)} fusion(bf16[1024,1]{0,1:T(2,128)(2,1)S(1)} %reshape.249, f32[1024]{0:T(1024)} %param.20, bf16[1024,1024]{1,0:T(8,128)(2,1)S(1)} %bitcast.325, bf16[1024,1024]{1,0:T(8,128)(2,1)} %param.19), kind=kOutput, calls=%fused_computation.1 | convolution fusion | flops 2152726528 | bytes 4204544 | tf_op jit(solution)/shard_map/dot_general | solution.py:13
  34.2 1.0 fusion.30
  35.2 0.9 fusion.29
  36.8 2.0 fusion.155
  39.2 1.8 fusion.13
  41.0 1.8 fusion.12
  42.9 1.8 fusion.11
  44.7 1.8 fusion.10
  46.6 0.9 fusion.9
  47.4 0.9 fusion.8
  48.3 0.9 fusion.7
  49.2 0.9 fusion.6
  50.1 55.1 %all-gather.3.cloned.1.call-done = bf16[7168,128]{1,0:T(8,128)(2,1)} async-done(((bf16[56,128]{1,0:T(8,128)(2,1)}), bf16[7168,128]{1,0:T(8,128)(2,1)}) %all-gather.3.cloned.1.call-update) | async-done | bytes 1835024 | tf_op jit(solution)/shard_map/all_gather | solution.py:17
  105.2 2.9 %fusion.164 = (bf16[128,1,128]{2,1,0:T(2,128)(2,1)S(1)}, bf16[128,1,128]{2,1,0:T(2,128)(2,1)S(1)}, bf16[128,1,128]{2,1,0:T(2,128)(2,1)S(1)}, bf16[128,1,128]{2,1...) fusion(bf16[128,56,128]{2,1,0:T(8,128)(2,1)} %bitcast.326), kind=kLoop, calls=%fused_computation.267 | loop fusion | bytes 524288 | tf_op jit(solution)/shard_map/slice | solution.py:106
  108.2 1.1 fusion.163
  112.1 1.4 multiply_convert_fusion
  114.9 46.5 %all-reduce.6.cloned.1.call-done = f32[392,128]{1,0:T(8,128)} async-done(((f32[392,128]{1,0:T(8,128)}), f32[392,128]{1,0:T(8,128)}) %all-reduce.6.cloned.1.call-update) | async-done | bytes 200720 | tf_op jit(solution)/shard_map/psum | solution.py:21
  161.4 1.7 fusion.53
  163.1 1.3 fusion.63
  164.4 1.3 fusion.76
  166.4 1.4 fusion.166
  168.7 50.7 %all-reduce.8.cloned.1.call-done = f32[520,128]{1,0:T(8,128)} async-done(((f32[520,128]{1,0:T(8,128)}), f32[520,128]{1,0:T(8,128)}) %all-reduce.8.cloned.1.call-update) | async-done | bytes 266256 | tf_op jit(solution)/shard_map/psum | solution.py:21
  220.2 1.3 fusion.20
  221.5 1.1 fusion.83
  222.5 1.9 add_multiply_fusion.1
  225.6 16.3 %all-to-all-start = ((f32[128,1,4]{2,1,0:T(1,128)}), f32[128,1,4]{2,1,0:T(1,128)S(1)}, u32[]{:S(2)}, u32[]{:S(2)}) async-start(f32[128,1,4]{2,1,0:T(1,128)} %copy.50), calls=%async_computation | async-start | bytes 131072 | tf_op jit(solution)/shard_map/all_to_all | solution.py:169
  241.9 11.4 %all-to-all-done = f32[128,1,4]{2,1,0:T(1,128)S(1)} async-done(((f32[128,1,4]{2,1,0:T(1,128)}), f32[128,1,4]{2,1,0:T(1,128)S(1)}, u32[]{:S(2)}, u32[]{:S(2)}) %all-to-all-start) | async-done | bytes 2080 | tf_op jit(solution)/shard_map/all_to_all | solution.py:169
  (69 shorter events, 13.6 us)
Async XLA Ops:
  6.5 23.1 %copy-start = (bf16[2,512,1024]{2,1,0:T(8,128)(2,1)S(1)}, bf16[2,512,1024]{2,1,0:T(8,128)(2,1)}, u32[]{:S(2)}) copy-start(bf16[2,512,1024]{2,1,0:T(8,128)(2,1)} %param.13) | copy-start | bytes 6291460
  6.5 98.7 %all-gather.3.cloned.1.call-start = ((), (), s32[]{:S(2)}) async-start(), calls=%async_computation.3 | async-start | bytes 1849344 | tf_op jit(solution)/shard_map/all_gather | solution.py:17
  16.4 144.9 %all-reduce.6.cloned.1.call-start = ((), (), s32[]{:S(2)}) async-start(), calls=%async_computation.1 | async-start | bytes 401408 | tf_op jit(solution)/shard_map/psum | solution.py:21
  29.6 4.4 %copy-start.3 = (s32[2,128]{1,0:T(2,128)S(1)}, s32[2,128]{1,0:T(2,128)}, u32[]{:S(2)}) copy-start(s32[2,128]{1,0:T(2,128)} %param.15) | copy-start | bytes 3076
  29.6 4.4 %copy-start.4 = (s32[2,1]{0,1:T(1,128)S(1)}, s32[2,1]{0,1:T(1,128)}, u32[]{:S(2)}) copy-start(s32[2,1]{0,1:T(1,128)} %param.16) | copy-start | bytes 28
  29.6 9.2 %copy-start.2 = (s32[2,128,1]{1,2,0:T(1,128)S(1)}, s32[2,128,1]{1,2,0:T(1,128)}, u32[]{:S(2)}) copy-start(s32[2,128,1]{1,2,0:T(1,128)} %param.17) | copy-start | bytes 3076
  34.1 12.4 %copy-start.5 = (bf16[2,128,4096]{2,1,0:T(8,128)(2,1)S(1)}, bf16[2,128,4096]{2,1,0:T(8,128)(2,1)}, u32[]{:S(2)}) copy-start(bf16[2,128,4096]{2,1,0:T(8,128)(2,1)} %param.14) | copy-start | bytes 6291460
  105.2 4.0 %copy-start.1 = (bf16[7168,128]{1,0:T(8,128)(2,1)S(1)}, bf16[7168,128]{1,0:T(8,128)(2,1)}, u32[]{:S(2)}) copy-start(bf16[7168,128]{1,0:T(8,128)(2,1)} %all-gather.3.cloned.1.call-done) | copy-start | bytes 5505028
  114.9 104.5 %all-reduce.8.cloned.1.call-start = ((), (), s32[]{:S(2)}) async-start(), calls=%async_computation.2 | async-start | bytes 532480 | tf_op jit(solution)/shard_map/psum | solution.py:21
  225.6 27.7 %all-to-all-start = ((f32[128,1,4]{2,1,0:T(1,128)}), f32[128,1,4]{2,1,0:T(1,128)S(1)}, u32[]{:S(2)}, u32[]{:S(2)}) async-start(f32[128,1,4]{2,1,0:T(1,128)} %copy.50), calls=%async_computation | async-start | bytes 131072 | tf_op jit(solution)/shard_map/all_to_all | solution.py:169
Sparse Core Ops, SparseCore 0:
  16.6 88.6 all-gather.2
  115.0 46.3 all-reduce.5
  166.5 52.7 all-reduce.7
where the time goes:
time: 262 us; the launch traced here: 261 us
  waiting for transfers between devices  164 us (63%)
  matrix products  45.1 us (17%)
  starting transfers between devices  16.4 us (6%)
  between operations  13.4 us (5%)
  local copies, waits for them, and re-layouts  12.4 us (5%)
  other arithmetic  9.7 us (4%)
    psum x2, waiting for transfers between devices, sum_segments(): return lax.psum(value, 'segment')  97.2 us
    all_gather x1, waiting for transfers between devices, gather_blocks(): return lax.all_gather(block, 'shard', axis=0, tiled=False)  55.1 us
    dot_general x45, matrix products, fdot(): return jnp.dot(a, b, preferred_element_type=F32, precision=precision)  42.6 us
    all_to_all x1, starting transfers between devices, local(): lax.all_to_all(outgoing, 'shard', split_axis=0, concat_axis=0, tiled=True)  16.3 us
    all_to_all x1, waiting for transfers between devices, local(): lax.all_to_all(outgoing, 'shard', split_axis=0, concat_axis=0, tiled=True)  11.4 us
  transfers between devices with their start and end apart: 4, of which 4 were waited for; matrix products, arithmetic and copies ran while one was open for 14% of the time, Pallas kernels for 0%

commit v1 on v0

--- a/solution.py
+++ b/solution.py
@@ -18,7 +18,7 @@
 
 
 def sum_segments(value):
-    return lax.psum(value, "segment")
+    return jnp.sum(lax.all_gather(value, "segment"), axis=0)
 
 
 def local(

time: 262 us -> 201 us (0.77)
  waiting for transfers between devices: 164 us -> 91.5 us
  blocking collectives: 0 us -> 12 us
    psum x2 -> x0, waiting for transfers between devices: 97.2 us -> none  [sum_segments(): return lax.psum(value, 'segment')]
    all_gather x0 -> x1, waiting for transfers between devices: none -> 24.7 us  [sum_segments(): return jnp.sum(lax.all_gather(value, 'segment'), axis=0)]
    all_gather x0 -> x1, blocking collectives: none -> 12 us  [sum_segments(): return jnp.sum(lax.all_gather(value, 'segment'), axis=0)]
  transfers between devices with their start and end apart: 4 -> 3, of which waited for: 4 -> 3; matrix products, arithmetic and copies ran while one was open for 14% -> 18% of each run, Pallas kernels for 0% -> 0%
where the time goes in v1:
time: 201 us; the launch traced here: 199 us
  waiting for transfers between devices  91.5 us (46%)
  matrix products  45 us (22%)
  starting transfers between devices  15.2 us (8%)
  between operations  13.7 us (7%)
  blocking collectives  12 us (6%)
  local copies, waits for them, and re-layouts  11.1 us (6%)
  other arithmetic  10.8 us (5%)
    all_gather x1, waiting for transfers between devices, gather_blocks(): return lax.all_gather(block, 'shard', axis=0, tiled=False)  55.3 us
    dot_general x45, matrix products, fdot(): return jnp.dot(a, b, preferred_element_type=F32, precision=precision)  42.4 us
    all_gather x1, waiting for transfers between devices, sum_segments(): return jnp.sum(lax.all_gather(value, 'segment'), axis=0)  24.7 us
    all_to_all x1, starting transfers between devices, local(): lax.all_to_all(outgoing, 'shard', split_axis=0, concat_axis=0, tiled=True)  15.2 us
    all_gather x1, blocking collectives, sum_segments(): return jnp.sum(lax.all_gather(value, 'segment'), axis=0)  12 us
    all_to_all x1, waiting for transfers between devices, local(): lax.all_to_all(outgoing, 'shard', split_axis=0, concat_axis=0, tiled=True)  11.4 us
  transfers between devices with their start and end apart: 3, of which 3 were waited for; matrix products, arithmetic and copies ran while one was open for 18% of the time, Pallas kernels for 0%

profile of v1, /device:TPU:1, one launch (start us, length us, event | category | flops | bytes accessed | tf_op | source)
XLA Modules:
  0.0 199.4 jit_solution(2755291711203793521)
XLA Ops:
  7.3 0.8 fusion.38
  8.1 0.8 fusion.40
  8.9 0.8 fusion.42
  9.7 0.8 fusion.44
  10.6 0.8 fusion.46
  11.4 0.8 fusion.48
  14.6 1.8 concatenate.25
  17.2 0.9 fusion.28
  18.0 0.9 fusion.27
  18.9 0.9 fusion.26
  19.8 0.9 fusion.25
  20.7 0.9 fusion.24
  21.6 0.9 fusion.23
  22.5 0.9 fusion.22
  23.4 0.9 fusion.21
  24.3 0.9 fusion.36
  25.1 0.9 fusion.35
  26.0 0.9 fusion.34
  26.9 0.9 fusion.33
  27.8 0.9 fusion.32
  28.7 4.4 %fusion = f32[1,1024]{1,0:T(1,128)S(1)} fusion(bf16[1024,1]{0,1:T(2,128)(2,1)S(1)} %reshape.251, f32[1024]{0:T(1024)} %param.20, bf16[1024,1024]{1,0:T(8,128)(2,1)S(1)} %bitcast.327, bf16[1024,1024]{1,0:T(8,128)(2,1)} %param.19), kind=kOutput, calls=%fused_computation.1 | convolution fusion | flops 2152726528 | bytes 4204544 | tf_op jit(solution)/shard_map/dot_general | solution.py:13
  33.1 0.9 fusion.31
  34.0 1.0 fusion.30
  35.1 0.9 fusion.29
  36.7 2.0 fusion.154
  39.0 1.8 fusion.13
  40.8 1.8 fusion.12
  42.6 1.8 fusion.11
  44.5 1.8 fusion.10
  46.3 0.9 fusion.9
  47.2 0.9 fusion.8
  48.1 0.9 fusion.7
  49.0 0.9 fusion.6
  49.9 55.3 %all-gather.6.cloned.1.call-done = bf16[7168,128]{1,0:T(8,128)(2,1)} async-done(((bf16[56,128]{1,0:T(8,128)(2,1)}), bf16[7168,128]{1,0:T(8,128)(2,1)}) %all-gather.6.cloned.1.call-update) | async-done | bytes 1835024 | tf_op jit(solution)/shard_map/all_gather | solution.py:17
  105.2 2.9 %fusion.162 = (bf16[128,1,128]{2,1,0:T(2,128)(2,1)S(1)}, bf16[128,1,128]{2,1,0:T(2,128)(2,1)S(1)}, bf16[128,1,128]{2,1,0:T(2,128)(2,1)S(1)}, bf16[128,1,128]{2,1...) fusion(bf16[128,56,128]{2,1,0:T(8,128)(2,1)} %bitcast.328), kind=kLoop, calls=%fused_computation.266 | loop fusion | bytes 524288 | tf_op jit(solution)/shard_map/slice | solution.py:106
  108.2 1.1 fusion.161
  112.0 1.4 multiply_convert_fusion
  114.1 12.0 %all-gather.1 = f32[1568,128]{1,0:T(8,128)S(1)} all-gather(f32[392,128]{1,0:T(8,128)S(1)} %pad.13), channel_id=3, replica_groups=mesh['segment'=4,'shard'=128] {'segment'}, dimensions={0}, use_global_device_ids=true | all-gather | bytes 1003520 | tf_op jit(solution)/shard_map/all_gather | solution.py:21
  126.8 1.7 fusion.53
  128.5 1.3 fusion.63
  129.8 1.3 fusion.76
  132.1 1.4 fusion.164
  134.3 24.7 %all-gather.8.cloned.1.call-done = f32[2080,128]{1,0:T(8,128)} async-done(((f32[520,128]{1,0:T(8,128)}), f32[2080,128]{1,0:T(8,128)}) %all-gather.8.cloned.1.call-update) | async-done | bytes 1064976 | tf_op jit(solution)/shard_map/all_gather | solution.py:21
  159.1 1.3 reduce_sum.143
  160.8 1.1 fusion.20
  161.9 1.9 add_multiply_fusion.1
  165.0 15.2 %all-to-all-start = ((f32[128,1,4]{2,1,0:T(1,128)}), f32[128,1,4]{2,1,0:T(1,128)S(1)}, u32[]{:S(2)}, u32[]{:S(2)}) async-start(f32[128,1,4]{2,1,0:T(1,128)} %copy.55), calls=%async_computation | async-start | bytes 131072 | tf_op jit(solution)/shard_map/all_to_all | solution.py:169
  180.2 11.4 %all-to-all-done = f32[128,1,4]{2,1,0:T(1,128)S(1)} async-done(((f32[128,1,4]{2,1,0:T(1,128)}), f32[128,1,4]{2,1,0:T(1,128)S(1)}, u32[]{:S(2)}, u32[]{:S(2)}) %all-to-all-start) | async-done | bytes 2080 | tf_op jit(solution)/shard_map/all_to_all | solution.py:169
  (73 shorter events, 13.2 us)
Async XLA Ops:
  6.5 22.2 %copy-start = (bf16[2,512,1024]{2,1,0:T(8,128)(2,1)S(1)}, bf16[2,512,1024]{2,1,0:T(8,128)(2,1)}, u32[]{:S(2)}) copy-start(bf16[2,512,1024]{2,1,0:T(8,128)(2,1)} %param.13) | copy-start | bytes 6291460
  6.5 98.7 %all-gather.6.cloned.1.call-start = ((), (), s32[]{:S(2)}) async-start(), calls=%async_computation.1 | async-start | bytes 1849344 | tf_op jit(solution)/shard_map/all_gather | solution.py:17
  16.4 142.6 %all-gather.8.cloned.1.call-start = ((), (), s32[]{:S(2)}) async-start(), calls=%async_computation.2 | async-start | bytes 1331200 | tf_op jit(solution)/shard_map/all_gather | solution.py:21
  28.7 10.0 %copy-start.3 = (s32[2,128]{1,0:T(2,128)S(1)}, s32[2,128]{1,0:T(2,128)}, u32[]{:S(2)}) copy-start(s32[2,128]{1,0:T(2,128)} %param.15) | copy-start | bytes 3076
  28.7 10.2 %copy-start.4 = (s32[2,1]{0,1:T(1,128)S(1)}, s32[2,1]{0,1:T(1,128)}, u32[]{:S(2)}) copy-start(s32[2,1]{0,1:T(1,128)} %param.16) | copy-start | bytes 28
  34.0 12.3 %copy-start.5 = (bf16[2,128,4096]{2,1,0:T(8,128)(2,1)S(1)}, bf16[2,128,4096]{2,1,0:T(8,128)(2,1)}, u32[]{:S(2)}) copy-start(bf16[2,128,4096]{2,1,0:T(8,128)(2,1)} %param.14) | copy-start | bytes 6291460
  48.1 61.8 %copy-start.2 = (s32[2,128,1]{1,2,0:T(1,128)S(1)}, s32[2,128,1]{1,2,0:T(1,128)}, u32[]{:S(2)}) copy-start(s32[2,128,1]{1,2,0:T(1,128)} %param.17) | copy-start | bytes 3076
  105.2 4.0 %copy-start.1 = (bf16[7168,128]{1,0:T(8,128)(2,1)S(1)}, bf16[7168,128]{1,0:T(8,128)(2,1)}, u32[]{:S(2)}) copy-start(bf16[7168,128]{1,0:T(8,128)(2,1)} %all-gather.6.cloned.1.call-done) | copy-start | bytes 5505028
  165.0 26.6 %all-to-all-start = ((f32[128,1,4]{2,1,0:T(1,128)}), f32[128,1,4]{2,1,0:T(1,128)S(1)}, u32[]{:S(2)}, u32[]{:S(2)}) async-start(f32[128,1,4]{2,1,0:T(1,128)} %copy.55), calls=%async_computation | async-start | bytes 131072 | tf_op jit(solution)/shard_map/all_to_all | solution.py:169
Sparse Core Ops, SparseCore 0:
  16.6 88.6 all-gather.5
  132.0 27.0 all-gather.7
